TPU v7x, 512 devices: a whole 4x4x16 slice. The times are simulated.
512 devices in a mesh: sub: 64 (over x, z), grp: 8 (over y, core).
Axes of the slice: x: 4, y: 4, z: 16, core: 2. Of those that a mesh axis runs over, the one named last changes fastest.
Arguments:
- rhs_jump: float32 [64, 8, 256, 256], P('sub', 'grp'), may hold values from -6 to 6
- incision: int32 [64, 8, 256], P('sub', 'grp'), may hold values 0 or 1
- precond: float32 [64, 8, 256], P('sub', 'grp'), may hold values from 0.5 to 2
- left_rows: int32 [64, 8, 256], P('sub', 'grp'), may hold values from 0 to 1151, as said below
- right_rows: int32 [64, 8, 256], P('sub', 'grp'), may hold values from 0 to 1151, as said below
- diag_inv: float32 [64, 8, 3, 384, 384], P('sub', 'grp'), as said below
- coupling: float32 [64, 8, 2, 384, 384], P('sub', 'grp'), may hold values from -0.09185587 to 0.09185587
- coarse_basis: float32 [64, 8, 3, 384, 128], P('sub', 'grp'), may hold values from -0.25 to 0.25
- coarse_inv: float32 [64, 128, 128], P('sub'), as said below
Outputs:
- multipliers: float32 [64, 8, 256, 256], P('sub', 'grp')
- residual: float32 [64, 8, 256, 256], P('sub', 'grp')
Inputs may be any that keep to these rules, and one draw needn't show every extreme that they name: `left_rows`: for each subdomain, its 256 left rows and 256 right rows are 512 distinct interior rows. `right_rows`: see left_rows. `diag_inv`: every block is invertible. `coarse_inv`: every block is symmetric positive definite.
All inputs are finite; a program needn't handle non-finite values. No bound on the sum of `incision` on one device may be relied on, other than what follows from the above.
Results may differ from a plain program's by a relative error of at most 0.0003.
Values sent between devices are 32-bit elements; how exact they have to be, the bound alone decides.
No kernel may reach another device: no remote copies, remote signals or barrier semaphores. Data moves between devices by JAX's collectives and lax.ppermute only.
A program may use at most 64 MiB of HBM per device.

v0:
```python
import jax
import jax.numpy as jnp
from jax import lax
from jax.sharding import PartitionSpec as P

ITERS = 3
HIGH = lax.Precision.HIGHEST


def passed_along(shard, axis, by):
    peers = lax.axis_size(axis)
    return lax.ppermute(shard, axis, [(i, (i + by) % peers) for i in range(peers)])


def norm_total(value):
    return lax.psum(value, ("sub", "grp"))


def local(
    rhs_jump, incision, precond, left_rows, right_rows, diag_inv, coupling, coarse_basis, coarse_inv
):
    load_rhs = rhs_jump[0, 0]
    cut = incision[0, 0].astype(jnp.float32)[:, None]
    scaling = precond[0, 0][:, None]
    lrow = left_rows[0, 0]
    rrow = right_rows[0, 0]
    dinv = diag_inv[0, 0]
    coup = coupling[0, 0]
    nblk, blk = (dinv.shape[0], dinv.shape[1])
    order = nblk * blk
    basis = coarse_basis[0, 0].reshape(order, -1)
    cinv = coarse_inv[0]
    width = load_rhs.shape[1]
    start = load_rhs[None]
    scales = scaling[None]
    cuts = cut[None]

    def local_dot(first, second):
        return jnp.sum(first[-1] * second[-1], axis=0)

    multipliers = jnp.zeros_like(start)
    residual = cuts * start
    zvec = scales * residual
    direc = zvec
    rz_now = norm_total(local_dot(residual, zvec))
    for step in range(ITERS):
        apply_own = direc[0]
        apply_left = passed_along(apply_own, "sub", 1)
        zeros = jnp.zeros((order, width), jnp.float32)
        interior_load = zeros.at[rrow].add(apply_own).at[lrow].add(-apply_left)
        primal = jnp.einsum("np,nr->pr", basis, interior_load, precision=HIGH)
        summed = lax.psum(primal, "grp")
        pieces = interior_load.reshape(nblk, blk, width)
        forward = []
        for block in range(nblk):
            rhs_now = pieces[block]
            if block > 0:
                rhs_now = rhs_now - jnp.dot(coup[block - 1], forward[-1], precision=HIGH)
            forward.append(jnp.dot(dinv[block], rhs_now, precision=HIGH))
        backward = [None] * nblk
        for block in range(nblk - 1, -1, -1):
            rhs_now = forward[block]
            if block < nblk - 1:
                rhs_now = rhs_now - jnp.dot(coup[block].T, backward[block + 1], precision=HIGH)
            backward[block] = jnp.dot(dinv[block].T, rhs_now, precision=HIGH)
        solved = jnp.concatenate(backward, axis=0)
        coarse = jnp.dot(cinv, summed, precision=HIGH)
        disp = solved + jnp.dot(basis, coarse, precision=HIGH)
        yleft = jnp.take(disp, lrow, axis=0)
        yright = jnp.take(disp, rrow, axis=0)
        nextone = passed_along(yleft, "sub", -1)
        image = (cut * (yright - nextone))[None]
        alpha = rz_now / lax.psum(local_dot(direc, image), ("sub", "grp"))
        multipliers = multipliers + alpha * direc
        residual = residual - alpha * image
        if step + 1 < ITERS:
            zvec = scales * residual
            rz_new = norm_total(local_dot(residual, zvec))
            direc = zvec + rz_new / rz_now * direc
            rz_now = rz_new
    return (multipliers[-1][None, None], residual[-1][None, None])


def solution(mesh):
    placed = (
        P("sub", "grp", None, None),
        P("sub", "grp", None),
        P("sub", "grp", None),
        P("sub", "grp", None),
        P("sub", "grp", None),
        P("sub", "grp", None, None, None),
        P("sub", "grp", None, None, None),
        P("sub", "grp", None, None, None),
        P("sub", None, None),
    )
    return jax.shard_map(
        local,
        mesh=mesh,
        in_specs=placed,
        out_specs=(P("sub", "grp", None, None), P("sub", "grp", None, None)),
        check_vma=False,
    )
```

profile of v0, /device:TPU:1, one launch (start us, length us, event | category | flops | bytes accessed | tf_op | source)
XLA Modules:
  0.0 924.1 jit_solution(12377833747426889409)
XLA Ops:
  9.1 4.4 collective-permute-start
  16.2 3.6 scatter_custom_fusion
  20.4 8.8 collective-permute-done
  29.9 4.7 scatter_custom_fusion.1
  51.8 67.6 %all-reduce.5.cloned.1.call-done = f32[128,256]{0,1:T(8,128)} async-done(((f32[128,256]{0,1:T(8,128)}), f32[128,256]{0,1:T(8,128)}) %all-reduce.5.cloned.1.call-update) | async-done | bytes 131088 | tf_op jit(solution)/shard_map/psum | solution.py:52
  120.6 3.3 fusion.2
  126.6 2.9 gather_fusion.1
  131.3 7.0 collective-permute-start.1
  139.7 2.9 gather_fusion
  144.5 106.5 %all-reduce = (f32[256]{0:T(256)}, f32[256]{0:T(256)}) all-reduce(f32[256]{0:T(256)} %get-tuple-element.4, f32[256]{0:T(256)S(1)} %get-tuple-element.3), channel_id=1, replica_groups=mesh['sub'=64,'grp'=8] {'sub','grp'}, use_global_device_ids=true, to_apply=%region_1.0 | all-reduce | flops 512 | bytes 4096 | tf_op jit(solution)/shard_map/psum | solution.py:16
  254.2 98.8 %psum.66 = f32[256]{0:T(256)S(1)} all-reduce(f32[256]{0:T(256)} %get-tuple-element.9), channel_id=1, replica_groups=mesh['sub'=64,'grp'=8] {'sub','grp'}, use_global_device_ids=true, to_apply=%region_8.10 | all-reduce | flops 256 | bytes 2048 | tf_op jit(solution)/shard_map/psum | solution.py:16
  355.5 3.7 collective-permute-start.2
  359.2 3.4 scatter_custom_fusion.2
  362.6 5.6 collective-permute-done.2
  368.3 4.9 scatter_custom_fusion.3
  373.1 3.3 fusion.43
  392.8 62.3 %all-reduce.7.cloned.1.call-done = f32[128,256]{0,1:T(8,128)} async-done(((f32[128,256]{0,1:T(8,128)}), f32[128,256]{0,1:T(8,128)}) %all-reduce.7.cloned.1.call-update) | async-done | bytes 131088 | tf_op jit(solution)/shard_map/psum | solution.py:52
  456.4 3.4 fusion.1
  462.4 3.0 gather_fusion.3
  467.2 7.0 collective-permute-start.3
  474.2 3.1 gather_fusion.2
  479.6 107.2 %psum.68 = f32[256]{0:T(256)} all-reduce(f32[256]{0:T(256)} %multiply_reduce_fusion.1), channel_id=1, replica_groups=mesh['sub'=64,'grp'=8] {'sub','grp'}, use_global_device_ids=true, to_apply=%region_13.15 | all-reduce | flops 256 | bytes 2048 | tf_op jit(solution)/shard_map/psum | solution.py:73
  590.6 98.5 %psum.69 = f32[256]{0:T(256)} all-reduce(f32[256]{0:T(256)} %get-tuple-element.7), channel_id=1, replica_groups=mesh['sub'=64,'grp'=8] {'sub','grp'}, use_global_device_ids=true, to_apply=%region_15.17 | all-reduce | flops 256 | bytes 2048 | tf_op jit(solution)/shard_map/psum | solution.py:16
  691.6 3.7 collective-permute-start.4
  695.3 3.4 scatter_custom_fusion.4
  698.7 5.7 collective-permute-done.4
  704.3 4.7 scatter_custom_fusion.5
  709.0 3.3 fusion.40
  725.9 3.0 convolution_bitcast_fusion.3
  728.8 62.6 %all-reduce.9.cloned.1.call-done = f32[128,256]{0,1:T(8,128)} async-done(((f32[128,256]{0,1:T(8,128)}), f32[128,256]{0,1:T(8,128)}) %all-reduce.9.cloned.1.call-update) | async-done | bytes 131088 | tf_op jit(solution)/shard_map/psum | solution.py:52
  796.5 7.1 collective-permute-start.5
  808.0 107.2 %psum.71 = f32[256]{0:T(256)S(1)} all-reduce(f32[256]{0:T(256)S(1)} %multiply_reduce_fusion), channel_id=1, replica_groups=mesh['sub'=64,'grp'=8] {'sub','grp'}, use_global_device_ids=true, to_apply=%region_20.22 | all-reduce | flops 256 | bytes 2048 | tf_op jit(solution)/shard_map/psum | solution.py:73
  (142 shorter events, 93.0 us)
Async XLA Ops:
  7.2 39.0 %copy-start = (f32[1,1,3,384,128]{4,3,2,1,0:T(8,128)S(1)}, f32[1,1,3,384,128]{4,3,2,1,0:T(8,128)}, u32[]{:S(2)}) copy-start(f32[1,1,3,384,128]{4,3,2,1,0:T(8,128)} %param.18) | copy-start | bytes 1769476
  7.2 12.7 %copy-start.31 = (s32[1,1,256]{2,1,0:T(1,128)S(1)}, s32[1,1,256]{2,1,0:T(1,128)}, u32[]{:S(2)}) copy-start(s32[1,1,256]{2,1,0:T(1,128)} %param.15) | copy-start | bytes 3076
  7.2 112.2 %all-reduce.5.cloned.1.call-start = ((), (), s32[]{:S(2)}) async-start(), calls=%async_computation | async-start | bytes 262144 | tf_op jit(solution)/shard_map/psum | solution.py:52
  9.1 20.1 %collective-permute-start = (f32[256,256]{1,0:T(8,128)S(1)}, f32[256,256]{1,0:T(8,128)S(1)}, u32[]{:S(2)}, u32[]{:S(2)}) collective-permute-start(f32[256,256]{1,0:T(8,128)S(1)} %fusion.98), channel_id=1, source_target_pairs={{0,8},{8,16},{16,24},{24,32},{32,40},{40,48},{48,56},{56,64},{64,7... | collective-permute-start | bytes 786440 | tf_op jit(solution)/shard_map/ppermute | solution.py:12
  14.1 20.5 %copy-start.32 = (s32[256,1]{0,1:T(1,128)}, s32[256,1]{0,1:T(1,128)S(1)}, u32[]{:S(2)}) copy-start(s32[256,1]{0,1:T(1,128)S(1)} %compare_select_fusion) | copy-start | bytes 3076
  15.5 114.1 %copy-start.29 = (pred[256]{0:T(512)(128)(4,1)}, pred[256]{0:T(512)(128)(4,1)S(1)}, u32[]{:S(2)}) copy-start(pred[256]{0:T(512)(128)(4,1)S(1)} %compare_and_fusion) | copy-start | bytes 772
  16.2 13.0 %copy-start.33 = (s32[256,1]{0,1:T(1,128)}, s32[256,1]{0,1:T(1,128)S(1)}, u32[]{:S(2)}) copy-start(s32[256,1]{0,1:T(1,128)S(1)} %compare_select_fusion.1) | copy-start | bytes 3076
  16.2 110.4 %copy-start.22 = (s32[1024]{0:T(1024)}, s32[1024]{0:T(1024)S(1)}, u32[]{:S(2)}) copy-start(s32[1024]{0:T(1024)S(1)} %pad_clamp_fusion) | copy-start | bytes 12292
  16.2 18.4 %copy-start.1 = (f32[1,1,3,384,384]{4,3,2,1,0:T(8,128)S(1)}, f32[1,1,3,384,384]{4,3,2,1,0:T(8,128)}, u32[]{:S(2)}) copy-start(f32[1,1,3,384,384]{4,3,2,1,0:T(8,128)} %param.16) | copy-start | bytes 5308420
  29.9 7.3 copy-start.2
  34.6 3.4 copy-start.7
  48.9 406.3 %all-reduce.7.cloned.1.call-start = ((), (), s32[]{:S(2)}) async-start(), calls=%async_computation.1 | async-start | bytes 262144 | tf_op jit(solution)/shard_map/psum | solution.py:52
  131.3 11.3 %collective-permute-start.1 = (f32[256,256]{1,0:T(8,128)}, f32[256,256]{1,0:T(8,128)}, u32[]{:S(2)}, u32[]{:S(2)}) collective-permute-start(f32[256,256]{1,0:T(8,128)} %broadcast_select_fusion.2), channel_id=1, source_target_pairs={{0,504},{8,0},{16,8},{24,16},{32,24},{40,32},{48,40},{56,48},{64,5... | collective-permute-start | bytes 786440 | tf_op jit(solution)/shard_map/ppermute | solution.py:12
  139.0 3.6 copy-start.23
  139.7 3.0 copy-start.21
  251.7 2.6 copy-start.25
  355.5 12.7 %collective-permute-start.2 = (f32[256,256]{1,0:T(8,128)}, f32[256,256]{1,0:T(8,128)}, u32[]{:S(2)}, u32[]{:S(2)}) collective-permute-start(f32[256,256]{1,0:T(8,128)} %multiply_add_fusion.1), channel_id=1, source_target_pairs={{0,8},{8,16},{16,24},{24,32},{32,40},{40,48},{48,56},{56,64},{64,7... | collective-permute-start | bytes 786440 | tf_op jit(solution)/shard_map/ppermute | solution.py:12
  373.1 3.3 copy-start.5
  385.7 2.6 copy-start.16
  390.0 401.5 %all-reduce.9.cloned.1.call-start = ((), (), s32[]{:S(2)}) async-start(), calls=%async_computation.2 | async-start | bytes 262144 | tf_op jit(solution)/shard_map/psum | solution.py:52
  467.2 10.6 %collective-permute-start.3 = (f32[256,256]{1,0:T(8,128)}, f32[256,256]{1,0:T(8,128)}, u32[]{:S(2)}, u32[]{:S(2)}) collective-permute-start(f32[256,256]{1,0:T(8,128)} %broadcast_select_fusion.1), channel_id=1, source_target_pairs={{0,504},{8,0},{16,8},{24,16},{32,24},{40,32},{48,40},{56,48},{64,5... | collective-permute-start | bytes 786440 | tf_op jit(solution)/shard_map/ppermute | solution.py:12
  691.6 12.7 %collective-permute-start.4 = (f32[256,256]{1,0:T(8,128)}, f32[256,256]{1,0:T(8,128)}, u32[]{:S(2)}, u32[]{:S(2)}) collective-permute-start(f32[256,256]{1,0:T(8,128)} %multiply_add_fusion), channel_id=1, source_target_pairs={{0,8},{8,16},{16,24},{24,32},{32,40},{40,48},{48,56},{56,64},{64,7... | collective-permute-start | bytes 786440 | tf_op jit(solution)/shard_map/ppermute | solution.py:12
  709.0 3.3 copy-start.3
  721.6 2.6 copy-start.17
  725.8 65.6 %copy-start.19 = (f32[1,128,128]{2,1,0:T(8,128)S(1)}, f32[1,128,128]{2,1,0:T(8,128)}, u32[]{:S(2)}) copy-start(f32[1,128,128]{2,1,0:T(8,128)} %param.19) | copy-start | bytes 196612
  725.8 66.8 %copy-start.13 = (f32[256,384]{1,0:T(8,128)S(1)}, f32[256,384]{1,0:T(8,128)}, u32[]{:S(2)}) copy-start(f32[256,384]{1,0:T(8,128)} %copy-done.12) | copy-start | bytes 1179652
  796.4 118.8 %copy-start.24 = (f32[256]{0:T(256)S(1)}, f32[256]{0:T(256)}, u32[]{:S(2)}) copy-start(f32[256]{0:T(256)} %psum.69) | copy-start | bytes 3076
  796.4 118.8 %copy-start.8 = (f32[1,1,256,256]{3,2,1,0:T(8,128)S(1)}, f32[1,1,256,256]{3,2,1,0:T(8,128)}, u32[]{:S(2)}) copy-start(f32[1,1,256,256]{3,2,1,0:T(8,128)} %param.11) | copy-start | bytes 786436
  796.5 118.8 %copy-start.18 = (f32[256,256]{1,0:T(8,128)S(1)}, f32[256,256]{1,0:T(8,128)}, u32[]{:S(2)}) copy-start(f32[256,256]{1,0:T(8,128)} %get-tuple-element.8) | copy-start | bytes 786436
  796.5 118.8 %copy-start.26 = (f32[256]{0:T(256)S(1)}, f32[256]{0:T(256)}, u32[]{:S(2)}) copy-start(f32[256]{0:T(256)} %copy-done.25) | copy-start | bytes 3076
  796.5 118.8 %copy-start.28 = (f32[256]{0:T(256)S(1)}, f32[256]{0:T(256)}, u32[]{:S(2)}) copy-start(f32[256]{0:T(256)} %copy-done.27) | copy-start | bytes 3076
  796.5 10.4 %collective-permute-start.5 = (f32[256,256]{1,0:T(8,128)S(1)}, f32[256,256]{1,0:T(8,128)S(1)}, u32[]{:S(2)}, u32[]{:S(2)}) collective-permute-start(f32[256,256]{1,0:T(8,128)S(1)} %broadcast_select_fusion), channel_id=1, source_target_pairs={{0,504},{8,0},{16,8},{24,16},{32,24},{40,32},{48,40},{56,48},{64,5... | collective-permute-start | bytes 786440 | tf_op jit(solution)/shard_map/ppermute | solution.py:12
  (11 other events, 14.9 us)
Sparse Core Ops, SparseCore 0:
  49.0 70.3 all-reduce.4
  390.1 65.0 all-reduce.6
  726.0 65.3 all-reduce.8
where the time goes:
time: 929 us; the launch traced here: 924 us
  blocking collectives  518 us (56%)
  waiting for transfers between devices  215 us (23%)
  matrix products  66.8 us (7%)
  other arithmetic  53 us (6%)
  starting transfers between devices  33.3 us (4%)
  local copies, waits for them, and re-layouts  22.8 us (2%)
  between operations  14.6 us (2%)
    psum x3, blocking collectives, norm_total(): return lax.psum(value, ('sub', 'grp'))  304 us
    psum x2, blocking collectives, local(): alpha = rz_now / lax.psum(local_dot(direc, image), ('sub', 'grp'))  214 us
    psum x3, waiting for transfers between devices, local(): summed = lax.psum(primal, 'grp')  192 us
    ppermute x6, starting transfers between devices, passed_along(): lax.ppermute(shard, axis, [(i, (i + by) % peers) for i in range(peers)])  32.8 us
    scatter-add x6, other arithmetic, local(): interior_load = zeros.at[rrow].add(apply_own).at[lrow].add(-apply_left)  24.6 us
    ppermute x6, waiting for transfers between devices, passed_along(): lax.ppermute(shard, axis, [(i, (i + by) % peers) for i in range(peers)])  22.8 us
  transfers between devices with their start and end apart: 9, of which 8 were waited for; matrix products, arithmetic and copies ran while one was open for 3% of the time, Pallas kernels for 0%

commit v1 on v0

--- a/solution.py
+++ b/solution.py
@@ -49,7 +49,7 @@
         zeros = jnp.zeros((order, width), jnp.float32)
         interior_load = zeros.at[rrow].add(apply_own).at[lrow].add(-apply_left)
         primal = jnp.einsum("np,nr->pr", basis, interior_load, precision=HIGH)
-        summed = lax.psum(primal, "grp")
+        summed = jnp.sum(lax.all_gather(primal, "grp"), axis=0)
         pieces = interior_load.reshape(nblk, blk, width)
         forward = []
         for block in range(nblk):

time: 929 us -> 770 us (0.83)
  waiting for transfers between devices: 215 us -> 57.4 us
  local copies, waits for them, and re-layouts: 22.8 us -> 41.7 us
  blocking collectives: 518 us -> 507 us
  matrix products: 66.8 us -> 56.8 us
    psum x3 -> x0, waiting for transfers between devices: 192 us -> none  [local(): summed = lax.psum(primal, 'grp')]
    all_gather x0 -> x3, waiting for transfers between devices: none -> 28.2 us  [local(): summed = jnp.sum(lax.all_gather(primal, 'grp'), axis=0)]
    unnamed x68 -> x105, local copies, waits for them, and re-layouts: 2.92 us -> 18.5 us
  transfers between devices with their start and end apart: 9 -> 9, of which waited for: 8 -> 9; matrix products, arithmetic and copies ran while one was open for 3% -> 9% of each run, Pallas kernels for 0% -> 0%
where the time goes in v1:
time: 770 us; the launch traced here: 764 us
  blocking collectives  507 us (66%)
  waiting for transfers between devices  57.4 us (7%)
  matrix products  56.8 us (7%)
  other arithmetic  50.1 us (7%)
  local copies, waits for them, and re-layouts  41.7 us (5%)
  starting transfers between devices  35.7 us (5%)
  between operations  15 us (2%)
    psum x3, blocking collectives, norm_total(): return lax.psum(value, ('sub', 'grp'))  301 us
    psum x2, blocking collectives, local(): alpha = rz_now / lax.psum(local_dot(direc, image), ('sub', 'grp'))  207 us
    ppermute x6, starting transfers between devices, passed_along(): lax.ppermute(shard, axis, [(i, (i + by) % peers) for i in range(peers)])  35.2 us
    ppermute x6, waiting for transfers between devices, passed_along(): lax.ppermute(shard, axis, [(i, (i + by) % peers) for i in range(peers)])  29.1 us
    all_gather x3, waiting for transfers between devices, local(): summed = jnp.sum(lax.all_gather(primal, 'grp'), axis=0)  28.2 us
    scatter-add x6, other arithmetic, local(): interior_load = zeros.at[rrow].add(apply_own).at[lrow].add(-apply_left)  21.1 us
    unnamed x105, local copies, waits for them, and re-layouts  18.5 us
  transfers between devices with their start and end apart: 9, of which 9 were waited for; matrix products, arithmetic and copies ran while one was open for 9% of the time, Pallas kernels for 0%

profile of v1, /device:TPU:1, one launch (start us, length us, event | category | flops | bytes accessed | tf_op | source)
XLA Modules:
  0.0 764.1 jit_solution(18404981242135431859)
XLA Ops:
  9.1 4.4 collective-permute-start
  19.5 9.6 %collective-permute-done = f32[256,256]{1,0:T(8,128)S(1)} collective-permute-done((f32[256,256]{1,0:T(8,128)S(1)}, f32[256,256]{1,0:T(8,128)S(1)}, u32[]{:S(2)}, u32[]{:S(2)}) %collective-permute-start) | collective-permute-done | bytes 262176 | tf_op jit(solution)/shard_map/ppermute | solution.py:12
  35.7 3.2 fusion.46
  52.9 10.3 %all-gather.7.cloned.1.call-done = f32[1024,256]{0,1:T(8,128)} async-done(((f32[128,256]{0,1:T(8,128)}), f32[1024,256]{0,1:T(8,128)}) %all-gather.7.cloned.1.call-update) | async-done | bytes 1048592 | tf_op jit(solution)/shard_map/all_gather | solution.py:52
  68.0 3.1 copy.40
  71.2 2.9 gather_fusion.1
  75.9 7.8 %collective-permute-start.1 = (f32[256,256]{1,0:T(8,128)}, f32[256,256]{1,0:T(8,128)}, u32[]{:S(2)}, u32[]{:S(2)}) collective-permute-start(f32[256,256]{1,0:T(8,128)} %broadcast_select_fusion.2), channel_id=1, source_target_pairs={{0,504},{8,0},{16,8},{24,16},{32,24},{40,32},{48,40},{56,48},{64,5... | collective-permute-start | bytes 786440 | tf_op jit(solution)/shard_map/ppermute | solution.py:12
  85.0 2.9 gather_fusion
  91.2 103.3 %all-reduce = (f32[256]{0:T(256)}, f32[256]{0:T(256)}) all-reduce(f32[256]{0:T(256)} %get-tuple-element.6, f32[256]{0:T(256)S(1)} %get-tuple-element.5), channel_id=1, replica_groups=mesh['sub'=64,'grp'=8] {'sub','grp'}, use_global_device_ids=true, to_apply=%region_1.0 | all-reduce | flops 512 | bytes 4096 | tf_op jit(solution)/shard_map/psum | solution.py:16
  197.7 98.7 %psum.44 = f32[256]{0:T(256)S(1)} all-reduce(f32[256]{0:T(256)} %get-tuple-element.11), channel_id=1, replica_groups=mesh['sub'=64,'grp'=8] {'sub','grp'}, use_global_device_ids=true, to_apply=%region_8.10 | all-reduce | flops 256 | bytes 2048 | tf_op jit(solution)/shard_map/psum | solution.py:16
  298.9 3.7 collective-permute-start.2
  302.6 3.4 scatter_custom_fusion.2
  306.0 5.6 collective-permute-done.2
  311.6 4.5 scatter_custom_fusion.3
  316.1 4.0 convolution_bitcast_fusion.13
  320.1 3.3 fusion.43
  338.5 9.0 %all-gather.9.cloned.1.call-done = f32[1024,256]{0,1:T(8,128)} async-done(((f32[128,256]{0,1:T(8,128)}), f32[1024,256]{0,1:T(8,128)}) %all-gather.9.cloned.1.call-update) | async-done | bytes 1048592 | tf_op jit(solution)/shard_map/all_gather | solution.py:52
  354.9 3.1 gather_fusion.3
  359.8 7.8 %collective-permute-start.3 = (f32[256,256]{1,0:T(8,128)}, f32[256,256]{1,0:T(8,128)}, u32[]{:S(2)}, u32[]{:S(2)}) collective-permute-start(f32[256,256]{1,0:T(8,128)} %broadcast_select_fusion.1), channel_id=1, source_target_pairs={{0,504},{8,0},{16,8},{24,16},{32,24},{40,32},{48,40},{56,48},{64,5... | collective-permute-start | bytes 786440 | tf_op jit(solution)/shard_map/ppermute | solution.py:12
  367.5 3.1 gather_fusion.2
  375.0 103.3 %psum.45 = f32[256]{0:T(256)} all-reduce(f32[256]{0:T(256)} %multiply_reduce_fusion.1), channel_id=1, replica_groups=mesh['sub'=64,'grp'=8] {'sub','grp'}, use_global_device_ids=true, to_apply=%region_13.15 | all-reduce | flops 256 | bytes 2048 | tf_op jit(solution)/shard_map/psum | solution.py:73
  482.0 98.8 %psum.46 = f32[256]{0:T(256)} all-reduce(f32[256]{0:T(256)} %get-tuple-element.9), channel_id=1, replica_groups=mesh['sub'=64,'grp'=8] {'sub','grp'}, use_global_device_ids=true, to_apply=%region_15.17 | all-reduce | flops 256 | bytes 2048 | tf_op jit(solution)/shard_map/psum | solution.py:16
  583.3 3.7 collective-permute-start.4
  586.9 3.4 scatter_custom_fusion.4
  590.3 5.7 collective-permute-done.4
  596.0 4.7 scatter_custom_fusion.5
  600.7 4.0 convolution_bitcast_fusion.12
  604.6 3.3 fusion.40
  623.1 8.9 %all-gather.11.cloned.1.call-done = f32[1024,256]{0,1:T(8,128)} async-done(((f32[128,256]{0,1:T(8,128)}), f32[1024,256]{0,1:T(8,128)}) %all-gather.11.cloned.1.call-update) | async-done | bytes 1048592 | tf_op jit(solution)/shard_map/all_gather | solution.py:52
  637.4 7.9 %collective-permute-start.5 = (f32[256,256]{1,0:T(8,128)S(1)}, f32[256,256]{1,0:T(8,128)S(1)}, u32[]{:S(2)}, u32[]{:S(2)}) collective-permute-start(f32[256,256]{1,0:T(8,128)S(1)} %broadcast_select_fusion), channel_id=1, source_target_pairs={{0,504},{8,0},{16,8},{24,16},{32,24},{40,32},{48,40},{56,48},{64,5... | collective-permute-start | bytes 786440 | tf_op jit(solution)/shard_map/ppermute | solution.py:12
  646.4 4.3 collective-permute-done.5
  651.8 103.3 %psum.47 = f32[256]{0:T(256)S(1)} all-reduce(f32[256]{0:T(256)S(1)} %multiply_reduce_fusion), channel_id=1, replica_groups=mesh['sub'=64,'grp'=8] {'sub','grp'}, use_global_device_ids=true, to_apply=%region_20.22 | all-reduce | flops 256 | bytes 2048 | tf_op jit(solution)/shard_map/psum | solution.py:73
  (185 shorter events, 104.3 us)
Async XLA Ops:
  7.2 25.5 %copy-start = (f32[1,1,3,384,128]{4,3,2,1,0:T(8,128)S(1)}, f32[1,1,3,384,128]{4,3,2,1,0:T(8,128)}, u32[]{:S(2)}) copy-start(f32[1,1,3,384,128]{4,3,2,1,0:T(8,128)} %param.18) | copy-start | bytes 1769476
  7.2 11.8 %copy-start.45 = (s32[1,1,256]{2,1,0:T(1,128)S(1)}, s32[1,1,256]{2,1,0:T(1,128)}, u32[]{:S(2)}) copy-start(s32[1,1,256]{2,1,0:T(1,128)} %param.15) | copy-start | bytes 3076
  7.2 56.0 %all-gather.7.cloned.1.call-start = ((), (), s32[]{:S(2)}) async-start(), calls=%async_computation | async-start | bytes 1179648 | tf_op jit(solution)/shard_map/all_gather | solution.py:52
  9.1 20.1 %collective-permute-start = (f32[256,256]{1,0:T(8,128)S(1)}, f32[256,256]{1,0:T(8,128)S(1)}, u32[]{:S(2)}, u32[]{:S(2)}) collective-permute-start(f32[256,256]{1,0:T(8,128)S(1)} %fusion.104), channel_id=1, source_target_pairs={{0,8},{8,16},{16,24},{24,32},{32,40},{40,48},{48,56},{56,64},{64,7... | collective-permute-start | bytes 786440 | tf_op jit(solution)/shard_map/ppermute | solution.py:12
  14.1 60.0 %copy-start.43 = (pred[256]{0:T(512)(128)(4,1)}, pred[256]{0:T(512)(128)(4,1)S(1)}, u32[]{:S(2)}) copy-start(pred[256]{0:T(512)(128)(4,1)S(1)} %compare_and_fusion) | copy-start | bytes 772
  15.5 16.1 %copy-start.46 = (s32[256,1]{0,1:T(1,128)}, s32[256,1]{0,1:T(1,128)S(1)}, u32[]{:S(2)}) copy-start(s32[256,1]{0,1:T(1,128)S(1)} %compare_select_fusion) | copy-start | bytes 3076
  16.2 15.5 %copy-start.47 = (s32[256,1]{0,1:T(1,128)}, s32[256,1]{0,1:T(1,128)S(1)}, u32[]{:S(2)}) copy-start(s32[256,1]{0,1:T(1,128)S(1)} %compare_select_fusion.1) | copy-start | bytes 3076
  16.2 55.0 %copy-start.36 = (s32[1024]{0:T(1024)}, s32[1024]{0:T(1024)S(1)}, u32[]{:S(2)}) copy-start(s32[1024]{0:T(1024)S(1)} %pad_clamp_fusion) | copy-start | bytes 12292
  31.6 3.7 copy-start.4
  32.7 3.0 copy-start.1
  35.4 7.4 copy-start.2
  35.4 312.0 %all-gather.9.cloned.1.call-start = ((), (), s32[]{:S(2)}) async-start(), calls=%async_computation.1 | async-start | bytes 1179648 | tf_op jit(solution)/shard_map/all_gather | solution.py:52
  42.8 2.0 copy-start.29
  75.9 13.5 %collective-permute-start.1 = (f32[256,256]{1,0:T(8,128)}, f32[256,256]{1,0:T(8,128)}, u32[]{:S(2)}, u32[]{:S(2)}) collective-permute-start(f32[256,256]{1,0:T(8,128)} %broadcast_select_fusion.2), channel_id=1, source_target_pairs={{0,504},{8,0},{16,8},{24,16},{32,24},{40,32},{48,40},{56,48},{64,5... | collective-permute-start | bytes 786440 | tf_op jit(solution)/shard_map/ppermute | solution.py:12
  84.3 3.6 copy-start.37
  85.0 4.3 copy-start.35
  195.2 2.6 copy-start.39
  298.9 12.7 %collective-permute-start.2 = (f32[256,256]{1,0:T(8,128)}, f32[256,256]{1,0:T(8,128)}, u32[]{:S(2)}, u32[]{:S(2)}) collective-permute-start(f32[256,256]{1,0:T(8,128)} %multiply_add_fusion.1), channel_id=1, source_target_pairs={{0,8},{8,16},{16,24},{24,32},{32,40},{40,48},{48,56},{56,64},{64,7... | collective-permute-start | bytes 786440 | tf_op jit(solution)/shard_map/ppermute | solution.py:12
  320.1 3.3 copy-start.5
  324.3 307.6 %all-gather.11.cloned.1.call-start = ((), (), s32[]{:S(2)}) async-start(), calls=%async_computation.2 | async-start | bytes 1179648 | tf_op jit(solution)/shard_map/all_gather | solution.py:52
  328.3 2.0 copy-start.30
  330.3 1.9 copy-start.27
  359.8 13.5 %collective-permute-start.3 = (f32[256,256]{1,0:T(8,128)}, f32[256,256]{1,0:T(8,128)}, u32[]{:S(2)}, u32[]{:S(2)}) collective-permute-start(f32[256,256]{1,0:T(8,128)} %broadcast_select_fusion.1), channel_id=1, source_target_pairs={{0,504},{8,0},{16,8},{24,16},{32,24},{40,32},{48,40},{56,48},{64,5... | collective-permute-start | bytes 786440 | tf_op jit(solution)/shard_map/ppermute | solution.py:12
  583.3 12.7 %collective-permute-start.4 = (f32[256,256]{1,0:T(8,128)}, f32[256,256]{1,0:T(8,128)}, u32[]{:S(2)}, u32[]{:S(2)}) collective-permute-start(f32[256,256]{1,0:T(8,128)} %multiply_add_fusion), channel_id=1, source_target_pairs={{0,8},{8,16},{16,24},{24,32},{32,40},{40,48},{48,56},{56,64},{64,7... | collective-permute-start | bytes 786440 | tf_op jit(solution)/shard_map/ppermute | solution.py:12
  604.6 3.3 copy-start.3
  612.7 2.0 copy-start.31
  637.3 117.8 %copy-start.38 = (f32[256]{0:T(256)S(1)}, f32[256]{0:T(256)}, u32[]{:S(2)}) copy-start(f32[256]{0:T(256)} %psum.46) | copy-start | bytes 3076
  637.4 117.8 %copy-start.6 = (f32[1,1,256,256]{3,2,1,0:T(8,128)S(1)}, f32[1,1,256,256]{3,2,1,0:T(8,128)}, u32[]{:S(2)}) copy-start(f32[1,1,256,256]{3,2,1,0:T(8,128)} %param.11) | copy-start | bytes 786436
  637.4 117.8 %copy-start.22 = (f32[256,256]{1,0:T(8,128)S(1)}, f32[256,256]{1,0:T(8,128)}, u32[]{:S(2)}) copy-start(f32[256,256]{1,0:T(8,128)} %get-tuple-element.10) | copy-start | bytes 786436
  637.4 117.8 %copy-start.40 = (f32[256]{0:T(256)S(1)}, f32[256]{0:T(256)}, u32[]{:S(2)}) copy-start(f32[256]{0:T(256)} %copy-done.39) | copy-start | bytes 3076
  637.4 117.8 %copy-start.42 = (f32[256]{0:T(256)S(1)}, f32[256]{0:T(256)}, u32[]{:S(2)}) copy-start(f32[256]{0:T(256)} %copy-done.41) | copy-start | bytes 3076
  637.4 13.3 %collective-permute-start.5 = (f32[256,256]{1,0:T(8,128)S(1)}, f32[256,256]{1,0:T(8,128)S(1)}, u32[]{:S(2)}, u32[]{:S(2)}) collective-permute-start(f32[256,256]{1,0:T(8,128)S(1)} %broadcast_select_fusion), channel_id=1, source_target_pairs={{0,504},{8,0},{16,8},{24,16},{32,24},{40,32},{48,40},{56,48},{64,5... | collective-permute-start | bytes 786440 | tf_op jit(solution)/shard_map/ppermute | solution.py:12
  (25 other events, 34.4 us)
Sparse Core Ops, SparseCore 0:
  35.5 27.6 all-gather.6
  324.4 22.9 all-gather.8
  609.0 22.9 all-gather.10
